TPU v7x, 32 devices: a whole 2x2x4 slice. The times are simulated.
32 devices in a mesh: seq: 8 (over y, x, core), pipe: 4 (over z).
Axes of the slice: x: 2, y: 2, z: 4, core: 2. Of those that a mesh axis runs over, the one named last changes fastest.
Arguments:
- query_in: bfloat16 [4, 1024, 4096], P('pipe', 'seq'), may hold values from -6 to 6
- key_in: bfloat16 [4, 1024, 4096], P('pipe', 'seq'), may hold values from -6 to 6
- value_in: bfloat16 [4, 1024, 4096], P('pipe', 'seq'), may hold values from -6 to 6
- grad_out: bfloat16 [4, 1024, 4096], P('pipe', 'seq'), may hold values from -6 to 6
- long_filter: float32 [4, 1024, 256], P('pipe', 'seq'), may hold values from -2 to 2, as said below
- short_taps: float32 [4, 3, 3, 4096], P('pipe'), may hold values from -3 to 3
Outputs:
- layer_out: bfloat16 [4, 1024, 4096], P('pipe', 'seq')
- passed_grads: bfloat16 [4, 3, 1024, 4096], P('pipe', None, 'seq')
- filter_grad: float32 [4, 1024, 256], P('pipe', 'seq')
- tap_grads: float32 [4, 3, 3, 4096], P('pipe')
Inputs may be any that keep to these rules, and one draw needn't show every extreme that they name: `long_filter`: one filter for each channel group of each section.
All inputs are finite; a program needn't handle non-finite values.
Results may differ from a plain program's by a relative error of at most 0.005.
Values may be sent and summed in bfloat16 or wider, within the bound.
No kernel may reach another device: no remote copies, remote signals or barrier semaphores. Data moves between devices by JAX's collectives and lax.ppermute only.
A program may use at most 256 MiB of HBM per device.

v0:
```python
import math
import jax
import jax.numpy as jnp
from jax import lax
from jax.sharding import PartitionSpec as P

exact_mode = lax.Precision.HIGHEST


def passed_along(x, axis, by):
    count = lax.axis_size(axis)
    pairs = [(i, i + by) for i in range(count) if 0 <= i + by < count]
    return lax.ppermute(x, axis, pairs)


def counting(length):
    return jnp.arange(length, dtype=jnp.int32)


def matmul(left, right):
    return jnp.dot(left, right, precision=exact_mode, preferred_element_type=jnp.float32)


def phases(row_index, col_index, modulus, direction):
    index_product = row_index[:, None] * col_index[None, :] % modulus
    phase_angle = index_product.astype(jnp.float32) * (-2.0 * math.pi * direction / modulus)
    return (jnp.cos(phase_angle), jnp.sin(phase_angle))


def complex_table(row_index, col_index, modulus, direction, factor):
    cosine_part, sine_part = phases(row_index, col_index, modulus, direction)
    upper = jnp.concatenate([cosine_part, -sine_part], axis=1)
    lower = jnp.concatenate([sine_part, cosine_part], axis=1)
    return jnp.concatenate([upper, lower], axis=0) * factor


def lead_segment(packed, row_index, col_index, modulus, direction, factor):
    in_shape = packed.shape
    flattened = packed.reshape(2 * in_shape[1], -1)
    table = complex_table(row_index, col_index, modulus, direction, factor)
    joined = matmul(table, flattened)
    return joined.reshape((2, row_index.shape[0]) + in_shape[2:])


def middle_segment(packed, row_index, col_index, modulus, direction):
    table = complex_table(row_index, col_index, modulus, direction, 1.0)
    table = table.reshape(2, row_index.shape[0], 2, col_index.shape[0])
    return jnp.einsum(
        "xrzb,zkbw->xkrw", table, packed, precision=exact_mode, preferred_element_type=jnp.float32
    )


def twiddle(packed, row_index, col_index, modulus, direction):
    cosine_part, sine_part = phases(row_index, col_index, modulus, direction)
    cosine_part = cosine_part[:, :, None]
    sine_part = sine_part[:, :, None]
    return jnp.stack(
        [
            packed[0] * cosine_part - packed[1] * sine_part,
            packed[0] * sine_part + packed[1] * cosine_part,
        ]
    )


def pack_pairs(values, pack_block):
    lead_dims = values.shape[:-1]
    split_view = values.reshape(lead_dims + (values.shape[-1] // (2 * pack_block), 2, pack_block))
    return jnp.stack(
        [
            split_view[..., 0, :].reshape(lead_dims + (-1,)),
            split_view[..., 1, :].reshape(lead_dims + (-1,)),
        ]
    )


def unpack_pairs(packed, pack_block):
    lead_dims = packed.shape[1:-1]
    pair_view = packed.reshape((2,) + lead_dims + (packed.shape[-1] // pack_block, pack_block))
    joined = jnp.stack([pair_view[0], pair_view[1]], axis=-2)
    return joined.reshape(lead_dims + (-1,))


def group_table(first_packed, col_count, half_group, groups):
    packed_index = first_packed + counting(col_count)
    return (packed_index[None, :] // half_group == counting(groups)[:, None]).astype(jnp.float32)


def spec_product(first_spec, second_spec):
    return jnp.stack(
        [
            first_spec[0] * second_spec[0] - first_spec[1] * second_spec[1],
            first_spec[0] * second_spec[1] + first_spec[1] * second_spec[0],
        ]
    )


def conj_product(first_spec, second_spec):
    return jnp.stack(
        [
            first_spec[0] * second_spec[0] + first_spec[1] * second_spec[1],
            first_spec[1] * second_spec[0] - first_spec[0] * second_spec[1],
        ]
    )


def spread_groups(spectrum, group_map):
    return jnp.einsum(
        "rktg,gq->rktq",
        spectrum,
        group_map,
        precision=exact_mode,
        preferred_element_type=jnp.float32,
    )


def sum_groups(spectrum, group_map):
    return jnp.einsum(
        "rktq,gq->rktg",
        spectrum,
        group_map,
        precision=exact_mode,
        preferred_element_type=jnp.float32,
    )


def local(query_in, key_in, value_in, grad_out, long_filter, short_taps):
    seq_size = lax.axis_size("seq")
    seq_rank = lax.axis_index("seq")
    rows_dev = query_in.shape[1]
    width = query_in.shape[2]
    groups = long_filter.shape[2]
    half_group = width // groups // 2
    pack_block = half_group // 2
    total_rows = rows_dev * seq_size
    fft_length = 2 * total_rows
    tap_table = short_taps[0]
    stacked_in = jnp.stack([query_in[0], key_in[0], value_in[0]])
    before = passed_along(stacked_in[:, rows_dev - 2 :, :], "seq", 1)
    extended = jnp.concatenate([before, stacked_in], axis=1).astype(jnp.float32)
    featured = tap_table[:, 0, None, :] * extended[:, 2 : 2 + rows_dev, :]
    featured = featured + tap_table[:, 1, None, :] * extended[:, 1 : 1 + rows_dev, :]
    featured = featured + tap_table[:, 2, None, :] * extended[:, 0:rows_dev, :]
    query_feat = featured[0]
    keyed = featured[1]
    valued = featured[2]
    grad_float = grad_out[0].astype(jnp.float32)
    product = (keyed * valued).astype(jnp.bfloat16)
    scaled = (grad_float * query_feat).astype(jnp.bfloat16)
    block_rows = rows_dev // seq_size
    group_map = group_table(0, width // 2, half_group, groups)
    freq_index = (
        (2 * seq_rank + counting(2))[:, None] + 2 * seq_size * counting(rows_dev)[None, :]
    ).reshape(-1)
    whole_filter = lax.all_gather(long_filter[0], "seq", axis=0, tiled=True)
    filter_cos, filter_sin = phases(freq_index, counting(total_rows), fft_length, 1)
    own_spec = jnp.stack(
        [matmul(filter_cos, whole_filter), matmul(filter_sin, whole_filter)]
    ).reshape(2, 2, rows_dev, groups)
    kernel = spread_groups(own_spec, group_map)

    def forward(signal):
        arrived = lax.all_to_all(signal[None], "seq", split_axis=1, concat_axis=0, tiled=True)
        packed = pack_pairs(arrived.astype(jnp.float32), pack_block)
        first_segment = lead_segment(
            packed, counting(2 * seq_size), counting(seq_size), 2 * seq_size, 1, 1.0
        )
        turned = twiddle(
            first_segment,
            counting(2 * seq_size),
            seq_rank * block_rows + counting(block_rows),
            fft_length,
            1,
        )
        gathered = lax.all_to_all(turned, "seq", split_axis=1, concat_axis=2, tiled=True)
        return middle_segment(gathered, counting(rows_dev), counting(rows_dev), rows_dev, 1)

    def inverse(spectrum):
        back_segment = middle_segment(
            spectrum, counting(rows_dev), counting(rows_dev), rows_dev, -1
        )
        turned = twiddle(
            back_segment, 2 * seq_rank + counting(2), counting(rows_dev), fft_length, -1
        )
        arrived = lax.all_to_all(turned, "seq", split_axis=2, concat_axis=1, tiled=True)
        row_data = lead_segment(
            arrived, counting(seq_size), counting(2 * seq_size), 2 * seq_size, -1, 1.0 / fft_length
        )
        spread_back = unpack_pairs(row_data, pack_block)
        return lax.all_to_all(spread_back, "seq", split_axis=0, concat_axis=1, tiled=True)[0]

    prod_spec = forward(product)
    conv_out = inverse(spec_product(prod_spec, kernel))
    scaled_spec = forward(scaled)
    back_out = inverse(conj_product(scaled_spec, kernel))
    cross_spec = sum_groups(conj_product(scaled_spec, prod_spec), group_map)
    cross_real = cross_spec[0].reshape(2 * rows_dev, groups)
    cross_imag = cross_spec[1].reshape(2 * rows_dev, groups)
    layer_out = (query_feat * conv_out).astype(jnp.bfloat16)
    grad_stack = jnp.stack([grad_float * conv_out, back_out * valued, back_out * keyed])
    after_rows = passed_along(grad_stack[:, :2, :].astype(jnp.bfloat16), "seq", -1).astype(
        jnp.float32
    )
    padded = jnp.concatenate([grad_stack, after_rows], axis=1)
    input_grads = tap_table[:, 0, None, :] * padded[:, 0:rows_dev, :]
    input_grads = input_grads + tap_table[:, 1, None, :] * padded[:, 1 : 1 + rows_dev, :]
    input_grads = input_grads + tap_table[:, 2, None, :] * padded[:, 2 : 2 + rows_dev, :]
    input_grads = input_grads.astype(jnp.bfloat16)
    tap_terms = jnp.stack(
        [
            jnp.sum(grad_stack * extended[:, 2 - tap_lag : 2 - tap_lag + rows_dev, :], axis=1)
            for tap_lag in range(3)
        ],
        axis=1,
    )
    tap_grads = lax.psum(tap_terms, "seq") / math.sqrt(total_rows)
    positions = counting(rows_dev * lax.axis_size("seq"))
    cosine_part, sine_part = phases(positions, freq_index, fft_length, -1)
    filter_grad = lax.psum_scatter(
        (matmul(cosine_part, cross_real) - matmul(sine_part, cross_imag)) / fft_length,
        "seq",
        scatter_dimension=0,
        tiled=True,
    ) / math.sqrt(total_rows * 2 * half_group)
    passed_grads = passed_along(input_grads, "pipe", -1)
    return (layer_out[None], passed_grads[None], filter_grad[None], tap_grads[None])


def solution(mesh):
    in_specs = (
        P("pipe", "seq", None),
        P("pipe", "seq", None),
        P("pipe", "seq", None),
        P("pipe", "seq", None),
        P("pipe", "seq", None),
        P("pipe", None, None, None),
    )
    out_specs = (
        P("pipe", "seq", None),
        P("pipe", None, "seq", None),
        P("pipe", "seq", None),
        P("pipe", None, None, None),
    )
    return jax.shard_map(local, mesh=mesh, in_specs=in_specs, out_specs=out_specs, check_vma=False)
```

profile of v0, /device:TPU:0, one launch (start us, length us, event | category | flops | bytes accessed | tf_op | source)
XLA Modules:
  0.0 850.4 jit_solution(6586171705041286776)
XLA Ops:
  20.4 7.1 reduce
  29.1 7.6 all-to-all-start.4
  36.9 15.1 %all-to-all-done.4 = bf16[8,2,32768]{2,1,0:T(2,128)(2,1)S(1)} async-done(((bf16[8,2,32768]{2,1,0:T(2,128)(2,1)}), bf16[8,2,32768]{2,1,0:T(2,128)(2,1)S(1)}, u32[]{:S(2)}, u32[]{:S(2)}) %all-to-all-start.4) | async-done | bytes 1048608 | tf_op jit(solution)/shard_map/all_to_all | solution.py:162
  57.9 8.5 reshape.367
  66.4 11.0 %fusion.148 = (f32[8,16,512,1,4]{1,0,4,3,2:T(8,128)}, f32[8,16,512,1,4]{1,0,4,3,2:T(8,128)}) fusion(f32[8,16,512,2,4]{1,0,4,3,2:T(8,128)} %reshape.367), kind=kLoop, calls=%fused_computation.231 | loop fusion | bytes 4194304 | tf_op jit(solution)/shard_map/slice | solution.py:70
  105.5 39.8 %all-gather.3.cloned.1.call-done = f32[1,1024,256]{2,1,0:T(8,128)} async-done(((f32[1,128,256]{2,1,0:T(8,128)}), f32[1,1024,256]{2,1,0:T(8,128)}) %all-gather.3.cloned.1.call-update) | async-done | bytes 1048592 | tf_op jit(solution)/shard_map/all_gather | solution.py:154
  164.6 7.1 fusion.18
  179.9 7.3 copy.194
  193.3 49.7 %all-to-all-done.6 = f32[2,2,128,2048]{3,0,1,2:T(2,128)} async-done(((f32[2,2,128,2048]{3,0,1,2:T(2,128)}), f32[2,2,128,2048]{3,0,1,2:T(2,128)}, u32[]{:S(2)}, u32[]{:S(2)}) %all-to-all-start.6) | async-done | bytes 4194336 | tf_op jit(solution)/shard_map/all_to_all | solution.py:184
  252.9 8.8 %copy.197 = f32[8,32768]{0,1:T(8,128)} copy(f32[8,32768]{1,0:T(8,128)S(1)} %get-tuple-element.37) | data formatting | bytes 2097152 | tf_op jit(solution)/shard_map/slice | solution.py:79
  261.7 8.8 %copy.198 = f32[8,32768]{0,1:T(8,128)} copy(f32[8,32768]{1,0:T(8,128)S(1)} %get-tuple-element.38) | data formatting | bytes 2097152 | tf_op jit(solution)/shard_map/slice | solution.py:79
  270.6 23.0 %pad_maximum_fusion.1 = f32[8,16,512,2,4]{0,4,2,1,3:T(4,128)} fusion(f32[8,16,512,1,4]{0,4,2,1,3:T(4,128)} %bitcast.249, f32[8,16,512,1,4]{0,4,2,1,3:T(4,128)} %bitcast.247), kind=kLoop, calls=%fused_computation.1 | loop fusion | flops 524288 | bytes 4194304 | tf_op jit(solution)/shard_map/stack | solution.py:79
  293.6 30.4 %copy.199 = f32[8,16,512,2,4]{1,0,4,3,2:T(8,128)} copy(f32[8,16,512,2,4]{0,4,2,1,3:T(4,128)} %pad_maximum_fusion.1) | data formatting | bytes 4194304 | tf_op jit(solution)/shard_map/stack | solution.py:79
  324.0 9.6 %copy.200 = f32[8,16,4096]{2,1,0:T(8,128)S(1)} copy(f32[8,16,4096]{1,0,2:T(8,128)} %bitcast.245) | data formatting | bytes 4194304 | tf_op jit(solution)/shard_map/reshape | solution.py:80
  333.6 29.4 %all_to_all.102 = f32[8,16,4096]{2,1,0:T(8,128)S(1)} all-to-all(f32[8,16,4096]{2,1,0:T(8,128)S(1)} %copy.200), channel_id=1, replica_groups=mesh['seq'=8,'pipe'=4] {'seq'}, dimensions={0} | all-to-all | bytes 4194304 | tf_op jit(solution)/shard_map/all_to_all | solution.py:189
  370.7 8.4 reduce.1
  380.7 18.8 %all_to_all.103 = bf16[8,2,32768]{2,1,0:T(2,128)(2,1)S(1)} all-to-all(bf16[8,2,32768]{2,1,0:T(2,128)(2,1)} %reshape.382), channel_id=1, replica_groups=mesh['seq'=8,'pipe'=4] {'seq'}, dimensions={0} | all-to-all | bytes 2097152 | tf_op jit(solution)/shard_map/all_to_all | solution.py:162
  410.5 10.6 %reshape.366 = f32[8,16,512,2,4]{1,0,4,3,2:T(8,128)} reshape(f32[1,128,4096]{1,2,0:T(8,128)} %copy.159) | data formatting | bytes 4194304 | tf_op jit(solution)/shard_map/convert_element_type | solution.py:163
  421.0 11.0 %fusion.149 = (f32[8,16,512,1,4]{1,0,4,3,2:T(8,128)}, f32[8,16,512,1,4]{1,0,4,3,2:T(8,128)}) fusion(f32[8,16,512,2,4]{1,0,4,3,2:T(8,128)} %reshape.366), kind=kLoop, calls=%fused_computation.232 | loop fusion | bytes 4194304 | tf_op jit(solution)/shard_map/slice | solution.py:70
  453.6 51.9 %all_to_all.104 = f32[2,16,16,2048]{3,2,0,1:T(8,128)S(1)} all-to-all(f32[2,16,16,2048]{3,2,0,1:T(8,128)S(1)} %pad_maximum_fusion.4), channel_id=1, replica_groups=mesh['seq'=8,'pipe'=4] {'seq'}, dimensions={1} | all-to-all | bytes 8388608 | tf_op jit(solution)/shard_map/all_to_all | solution.py:174
  506.5 8.3 fusion.15
  528.0 7.3 copy.173
  535.3 52.8 %all_to_all.105 = f32[2,2,128,2048]{3,0,1,2:T(2,128)S(1)} all-to-all(f32[2,2,128,2048]{3,0,1,2:T(2,128)} %copy.173), channel_id=1, replica_groups=mesh['seq'=8,'pipe'=4] {'seq'}, dimensions={2} | all-to-all | bytes 8388608 | tf_op jit(solution)/shard_map/all_to_all | solution.py:184
  596.7 9.1 %copy.176 = f32[8,32768]{0,1:T(8,128)} copy(f32[8,32768]{1,0:T(8,128)} %get-tuple-element.39) | data formatting | bytes 2097152 | tf_op jit(solution)/shard_map/slice | solution.py:79
  605.8 8.8 %copy.177 = f32[8,32768]{0,1:T(8,128)} copy(f32[8,32768]{1,0:T(8,128)S(1)} %get-tuple-element.40) | data formatting | bytes 2097152 | tf_op jit(solution)/shard_map/slice | solution.py:79
  614.7 23.0 %pad_maximum_fusion = f32[8,16,512,2,4]{0,4,2,1,3:T(4,128)} fusion(f32[8,16,512,1,4]{0,4,2,1,3:T(4,128)} %bitcast.250, f32[8,16,512,1,4]{0,4,2,1,3:T(4,128)} %bitcast.248), kind=kLoop, calls=%fused_computation | loop fusion | flops 524288 | bytes 4194304 | tf_op jit(solution)/shard_map/stack | solution.py:79
  637.7 30.4 %copy.178 = f32[8,16,512,2,4]{1,0,4,3,2:T(8,128)} copy(f32[8,16,512,2,4]{0,4,2,1,3:T(4,128)} %pad_maximum_fusion) | data formatting | bytes 4194304 | tf_op jit(solution)/shard_map/stack | solution.py:79
  668.1 10.6 %copy.179 = f32[8,16,4096]{2,1,0:T(8,128)} copy(f32[8,16,4096]{1,0,2:T(8,128)} %bitcast.246) | data formatting | bytes 4194304 | tf_op jit(solution)/shard_map/reshape | solution.py:80
  690.1 19.8 %all-to-all-done.3 = f32[8,16,4096]{2,1,0:T(8,128)} async-done(((f32[8,16,4096]{2,1,0:T(8,128)}), f32[8,16,4096]{2,1,0:T(8,128)}, u32[]{:S(2)}, u32[]{:S(2)}) %all-to-all-start.3) | async-done | bytes 2097184 | tf_op jit(solution)/shard_map/all_to_all | solution.py:189
  720.9 9.4 %multiply_reduce_fusion.2 = (f32[3,4096]{1,0:T(4,128)S(1)}, f32[3,4096]{1,0:T(4,128)S(1)}, f32[3,4096]{1,0:T(4,128)S(1)}, bf16[3,128,4096]{2,1,0:T(8,128)(2,1)}) fusion(f32[3,130,4096]{2,1,0:T(8,128)S(1)} %bitcast.244, f32[1,128,4096]{2,1,0:T(8,128)} %get-tuple-element.14, f32[1,128,4096]{2,1,0:T(8,128)S(1)} %get-tuple-element.13, ...), kind=kLoop, calls=%fused_computation.11 | loop fusion | flops 21983232 | bytes 41189376 | tf_op jit(solution)/shard_map/reduce_sum | solution.py:210
  745.0 38.3 %reduce-scatter.2.cloned.1.call-done = f32[128,256]{1,0:T(8,128)} async-done(((f32[1024,256]{1,0:T(8,128)}), f32[128,256]{1,0:T(8,128)}) %reduce-scatter.2.cloned.1.call-update) | async-done | bytes 131088 | tf_op jit(solution)/shard_map/reduce_scatter | solution.py:218
  784.8 55.2 %all-reduce.2.cloned.1.call-done = f32[3,3,4096]{2,1,0:T(4,128)} async-done(((f32[3,3,4096]{2,1,0:T(4,128)}), f32[3,3,4096]{2,1,0:T(4,128)}) %all-reduce.2.cloned.1.call-update) | async-done | bytes 147472 | tf_op jit(solution)/shard_map/psum | solution.py:215
  (181 shorter events, 198.1 us)
Async XLA Ops:
  7.2 5.3 copy-start.23
  10.0 3.3 collective-permute-start
  17.0 2.8 copy-start.5
  29.1 22.9 %all-to-all-start.4 = ((bf16[8,2,32768]{2,1,0:T(2,128)(2,1)}), bf16[8,2,32768]{2,1,0:T(2,128)(2,1)S(1)}, u32[]{:S(2)}, u32[]{:S(2)}) async-start(bf16[8,2,32768]{2,1,0:T(2,128)(2,1)} %reshape.384), calls=%async_computation.4 | async-start | bytes 2097152 | tf_op jit(solution)/shard_map/all_to_all | solution.py:162
  98.5 63.6 %all-to-all-start.5 = ((f32[2,16,16,2048]{3,2,0,1:T(8,128)}), f32[2,16,16,2048]{3,2,0,1:T(8,128)}, u32[]{:S(2)}, u32[]{:S(2)}) async-start(f32[2,16,16,2048]{3,2,0,1:T(8,128)} %pad_maximum_fusion.6), calls=%async_computation.5 | async-start | bytes 8388608 | tf_op jit(solution)/shard_map/all_to_all | solution.py:174
  103.1 42.3 %all-gather.3.cloned.1.call-start = ((), (), s32[]{:S(2)}) async-start(), calls=%async_computation.11 | async-start | bytes 1179648 | tf_op jit(solution)/shard_map/all_gather | solution.py:154
  104.6 60.0 %copy-start.10 = (f32[2,128,2,128]{3,2,1,0:T(2,128)}, f32[2,128,2,128]{3,2,1,0:T(2,128)S(1)}, u32[]{:S(2)}) copy-start(f32[2,128,2,128]{3,2,1,0:T(2,128)S(1)} %reshape.359) | copy-start | bytes 786436
  105.3 68.5 %copy-start.12 = (f32[2,128,2,128]{3,2,1,0:T(2,128)}, f32[2,128,2,128]{3,2,1,0:T(2,128)S(1)}, u32[]{:S(2)}) copy-start(f32[2,128,2,128]{3,2,1,0:T(2,128)S(1)} %reshape.360) | copy-start | bytes 786436
  105.3 53.1 %copy-start.24 = (s32[2048]{0:T(1024)}, s32[2048]{0:T(1024)S(1)}, u32[]{:S(2)}) copy-start(s32[2048]{0:T(1024)S(1)} %add_select_fusion.3) | copy-start | bytes 24580
  105.4 53.0 %copy-start.26 = (s32[256]{0:T(256)}, s32[256]{0:T(256)S(1)}, u32[]{:S(2)}) copy-start(s32[256]{0:T(256)S(1)} %add_bitcast_fusion) | copy-start | bytes 3076
  145.4 6.3 copy-start.28
  164.6 7.1 copy-start.1
  187.3 55.8 %all-to-all-start.6 = ((f32[2,2,128,2048]{3,0,1,2:T(2,128)}), f32[2,2,128,2048]{3,0,1,2:T(2,128)}, u32[]{:S(2)}, u32[]{:S(2)}) async-start(f32[2,2,128,2048]{3,0,1,2:T(2,128)} %copy.194), calls=%async_computation.6 | async-start | bytes 8388608 | tf_op jit(solution)/shard_map/all_to_all | solution.py:184
  506.5 8.3 copy-start.2
  506.5 8.3 copy-start.4
  514.8 5.4 copy-start.13
  678.7 4.8 copy-start.25
  678.7 31.1 %all-to-all-start.3 = ((f32[8,16,4096]{2,1,0:T(8,128)}), f32[8,16,4096]{2,1,0:T(8,128)}, u32[]{:S(2)}, u32[]{:S(2)}) async-start(f32[8,16,4096]{2,1,0:T(8,128)} %copy.179), calls=%async_computation.3 | async-start | bytes 4194304 | tf_op jit(solution)/shard_map/all_to_all | solution.py:189
  683.2 100.1 %reduce-scatter.2.cloned.1.call-start = ((), (), s32[]{:S(2)}) async-start(), calls=%async_computation.9 | async-start | bytes 1179648 | tf_op jit(solution)/shard_map/reduce_scatter | solution.py:218
  683.5 26.4 %copy-start.9 = (bf16[1,128,4096]{2,1,0:T(8,128)(2,1)S(1)}, bf16[1,128,4096]{2,1,0:T(8,128)(2,1)}, u32[]{:S(2)}) copy-start(bf16[1,128,4096]{2,1,0:T(8,128)(2,1)} %param.9) | copy-start | bytes 3145732
  709.8 3.8 copy-start.6
  713.6 4.2 copy-start.7
  713.6 7.3 slice-start
  714.3 3.4 collective-permute-start.1
  717.8 3.1 slice-start.1
  717.8 3.1 copy-start.16
  717.8 3.1 copy-start.18
  717.8 3.1 copy-start.20
  720.9 11.1 %copy-start.27 = (s32[256]{0:T(256)S(1)}, s32[256]{0:T(256)}, u32[]{:S(2)}) copy-start(s32[256]{0:T(256)} %copy-done.26) | copy-start | bytes 3076
  730.3 7.4 copy-start.22
  730.3 111.5 %collective-permute-start.2 = (bf16[3,128,4096]{2,1,0:T(8,128)(2,1)}, bf16[3,128,4096]{2,1,0:T(8,128)(2,1)S(1)}, u32[]{:S(2)}, u32[]{:S(2)}) collective-permute-start(bf16[3,128,4096]{2,1,0:T(8,128)(2,1)} %get-tuple-element.19), channel_id=1, source_target_pairs={{1,0},{2,1},{3,2},{5,4},{6,5},{7,6},{9,8},{10,9},{11,10},{13,12},{... | collective-permute-start | bytes 9437192 | tf_op jit(solution)/shard_map/ppermute | solution.py:13
  743.9 96.1 %all-reduce.2.cloned.1.call-start = ((), (), s32[]{:S(2)}) async-start(), calls=%async_computation.10 | async-start | bytes 393216 | tf_op jit(solution)/shard_map/psum | solution.py:215
  (9 other events, 18.0 us)
Sparse Core Ops, SparseCore 0:
  105.8 39.5 all-gather.2
  744.0 39.1 reduce-scatter.1
  786.3 53.6 all-reduce.1
where the time goes:
time: 862 us; the launch traced here: 850 us
  local copies, waits for them, and re-layouts  248 us (29%)
  waiting for transfers between devices  220 us (26%)
  blocking collectives  153 us (18%)
  other arithmetic  116 us (13%)
  matrix products  70.2 us (8%)
  starting transfers between devices  29 us (3%)
  between operations  15.1 us (2%)
    another operation x2, local copies, waits for them, and re-layouts, unpack_pairs(): joined = jnp.stack([pair_view[0], pair_view[1]], axis=-2)  60.9 us
    psum x1, waiting for transfers between devices, local(): tap_grads = lax.psum(tap_terms, 'seq') / math.sqrt(total_rows)  55.2 us
    all_to_all x1, blocking collectives, inverse(): lax.all_to_all(turned, 'seq', split_axis=2, concat_axis=1, tiled=True)  52.8 us
    all_to_all x1, blocking collectives, forward(): lax.all_to_all(turned, 'seq', split_axis=1, concat_axis=2, tiled=True)  51.9 us
    all_to_all x1, waiting for transfers between devices, inverse(): lax.all_to_all(turned, 'seq', split_axis=2, concat_axis=1, tiled=True)  49.7 us
    another operation x2, other arithmetic, unpack_pairs(): joined = jnp.stack([pair_view[0], pair_view[1]], axis=-2)  46 us
    all_gather x1, waiting for transfers between devices, local(): whole_filter = lax.all_gather(long_filter[0], 'seq', axis=0, tiled=True)  39.8 us
    reduce_scatter x1, waiting for transfers between devices, local(): lax.psum_scatter((matmul(cosine_part, cross_real) - matmul(sine_part, cro...  38.3 us
  transfers between devices with their start and end apart: 10, of which 8 were waited for; matrix products, arithmetic and copies ran while one was open for 5% of the time, Pallas kernels for 0%

commit v1 on v0

--- a/solution.py
+++ b/solution.py
@@ -5,6 +5,28 @@
 from jax.sharding import PartitionSpec as P
 
 exact_mode = lax.Precision.HIGHEST
+
+
+def cut_along(shard, dim, peers):
+    before, after = (shard.shape[:dim], shard.shape[dim + 1 :])
+    return jnp.moveaxis(shard.reshape(*before, peers, -1, *after), dim, 0)
+
+
+def joined_along(parts, dim):
+    lengths = list(parts.shape[1:])
+    lengths[dim] *= parts.shape[0]
+    return jnp.moveaxis(parts, 0, dim).reshape(lengths)
+
+
+def pairwise_exchange(array, axis, split_dim, concat_dim):
+    size, index = (lax.axis_size(axis), lax.axis_index(axis))
+    pieces = cut_along(array, split_dim, size)
+    done = [pieces[index]]
+    for step in range(1, size):
+        sent = pieces[index ^ step]
+        done.append(lax.ppermute(sent, axis, [(i, i ^ step) for i in range(size)]))
+    pieces = jnp.stack(done)[index ^ jnp.arange(size)]
+    return joined_along(pieces, concat_dim)
 
 
 def passed_along(x, axis, by):
@@ -171,7 +193,7 @@
             fft_length,
             1,
         )
-        gathered = lax.all_to_all(turned, "seq", split_axis=1, concat_axis=2, tiled=True)
+        gathered = pairwise_exchange(turned, "seq", 1, 2)
         return middle_segment(gathered, counting(rows_dev), counting(rows_dev), rows_dev, 1)
 
     def inverse(spectrum):

time: 862 us -> 887 us (1.029)
  blocking collectives: 153 us -> 101 us
  waiting for transfers between devices: 220 us -> 256 us
  local copies, waits for them, and re-layouts: 248 us -> 278 us
  other arithmetic: 116 us -> 128 us
    ppermute x0 -> x14, waiting for transfers between devices: none -> 81.2 us  [pairwise_exchange(): done.append(lax.ppermute(sent, axis, [(i, i ^ step) for i in range(size)]))]
    all_to_all x1 -> x0, blocking collectives: 51.9 us -> none  [forward(): lax.all_to_all(turned, 'seq', split_axis=1, concat_axis=2, tiled=True)]
    all_gather x1, waiting for transfers between devices: 39.8 us -> 0.01 us  [local(): whole_filter = lax.all_gather(long_filter[0], 'seq', axis=0, tiled=True)]
    unnamed x81 -> x113, local copies, waits for them, and re-layouts: 28.1 us -> 43.9 us
    ppermute x0 -> x14, starting transfers between devices: none -> 11.1 us  [pairwise_exchange(): done.append(lax.ppermute(sent, axis, [(i, i ^ step) for i in range(size)]))]
    gather x0 -> x2, local copies, waits for them, and re-layouts: none -> 10 us  [pairwise_exchange(): pieces = jnp.stack(done)[index ^ jnp.arange(size)]]
    unnamed x5 -> x7, other arithmetic: 17.1 us -> 18.7 us
  transfers between devices with their start and end apart: 10 -> 23, of which waited for: 8 -> 11; matrix products, arithmetic and copies ran while one was open for 5% -> 15% of each run, Pallas kernels for 0% -> 0%
where the time goes in v1:
time: 887 us; the launch traced here: 880 us
  local copies, waits for them, and re-layouts  278 us (31%)
  waiting for transfers between devices  256 us (29%)
  other arithmetic  128 us (14%)
  blocking collectives  101 us (11%)
  matrix products  70.5 us (8%)
  starting transfers between devices  31.2 us (4%)
  between operations  15 us (2%)
    ppermute x14, waiting for transfers between devices, pairwise_exchange(): done.append(lax.ppermute(sent, axis, [(i, i ^ step) for i in range(size)]))  81.2 us
    another operation x2, local copies, waits for them, and re-layouts, unpack_pairs(): joined = jnp.stack([pair_view[0], pair_view[1]], axis=-2)  61 us
    psum x1, waiting for transfers between devices, local(): tap_grads = lax.psum(tap_terms, 'seq') / math.sqrt(total_rows)  55.2 us
    all_to_all x1, blocking collectives, inverse(): lax.all_to_all(turned, 'seq', split_axis=2, concat_axis=1, tiled=True)  53.1 us
    all_to_all x1, waiting for transfers between devices, inverse(): lax.all_to_all(turned, 'seq', split_axis=2, concat_axis=1, tiled=True)  49 us
    another operation x2, other arithmetic, unpack_pairs(): joined = jnp.stack([pair_view[0], pair_view[1]], axis=-2)  45.1 us
    unnamed x113, local copies, waits for them, and re-layouts  43.9 us
    reduce_scatter x1, waiting for transfers between devices, local(): lax.psum_scatter((matmul(cosine_part, cross_real) - matmul(sine_part, cro...  38.3 us
  transfers between devices with their start and end apart: 23, of which 11 were waited for; matrix products, arithmetic and copies ran while one was open for 15% of the time, Pallas kernels for 0%

profile of v1, /device:TPU:0, one launch (start us, length us, event | category | flops | bytes accessed | tf_op | source)
XLA Modules:
  0.0 880.3 jit_solution(14971334951093697117)
XLA Ops:
  49.8 10.3 %all-to-all-done.3 = bf16[8,2,32768]{2,1,0:T(2,128)(2,1)S(1)} async-done(((bf16[8,2,32768]{2,1,0:T(2,128)(2,1)}), bf16[8,2,32768]{2,1,0:T(2,128)(2,1)S(1)}, u32[]{:S(2)}, u32[]{:S(2)}) %all-to-all-start.3) | async-done | bytes 1048608 | tf_op jit(solution)/shard_map/all_to_all | solution.py:184
  66.1 8.5 reshape.451
  74.7 11.1 %fusion.168 = (f32[8,16,512,1,4]{1,0,4,3,2:T(8,128)}, f32[8,16,512,1,4]{1,0,4,3,2:T(8,128)}) fusion(f32[8,16,512,2,4]{1,0,4,3,2:T(8,128)} %reshape.451), kind=kLoop, calls=%fused_computation.301 | loop fusion | bytes 4194304 | tf_op jit(solution)/shard_map/slice | solution.py:92
  117.8 18.0 %collective-permute-done.9 = f32[2,2,16,2048]{3,2,1,0:T(8,128)S(1)} collective-permute-done((f32[2,2,16,2048]{3,2,1,0:T(8,128)S(1)}, f32[2,2,16,2048]{3,2,1,0:T(8,128)S(1)}, u32[]{:S(2)}, u32[]{:S(2)}) %collective-permute-start.9) | collective-permute-done | bytes 524320 | tf_op jit(solution)/shard_map/ppermute | solution.py:27
  136.7 20.7 %collective-permute-done.10 = f32[2,2,16,2048]{3,2,1,0:T(8,128)S(1)} collective-permute-done((f32[2,2,16,2048]{3,2,1,0:T(8,128)S(1)}, f32[2,2,16,2048]{3,2,1,0:T(8,128)S(1)}, u32[]{:S(2)}, u32[]{:S(2)}) %collective-permute-start.10) | collective-permute-done | bytes 524320 | tf_op jit(solution)/shard_map/ppermute | solution.py:27
  169.1 8.7 fusion.18
  201.3 7.3 copy.164
  213.5 49.0 %all-to-all-done.4 = f32[2,2,128,2048]{3,0,1,2:T(2,128)} async-done(((f32[2,2,128,2048]{3,0,1,2:T(2,128)}), f32[2,2,128,2048]{3,0,1,2:T(2,128)}, u32[]{:S(2)}, u32[]{:S(2)}) %all-to-all-start.4) | async-done | bytes 4194336 | tf_op jit(solution)/shard_map/all_to_all | solution.py:206
  272.3 8.9 %copy.167 = f32[8,32768]{0,1:T(8,128)} copy(f32[8,32768]{1,0:T(8,128)S(1)} %get-tuple-element.49) | data formatting | bytes 2097152 | tf_op jit(solution)/shard_map/slice | solution.py:101
  281.2 8.9 %copy.168 = f32[8,32768]{0,1:T(8,128)} copy(f32[8,32768]{1,0:T(8,128)S(1)} %get-tuple-element.50) | data formatting | bytes 2097152 | tf_op jit(solution)/shard_map/slice | solution.py:101
  290.1 22.6 %pad_maximum_fusion.1 = f32[8,16,512,2,4]{0,4,2,1,3:T(4,128)} fusion(f32[8,16,512,1,4]{0,4,2,1,3:T(4,128)} %bitcast.227, f32[8,16,512,1,4]{0,4,2,1,3:T(4,128)} %bitcast.225), kind=kLoop, calls=%fused_computation.3 | loop fusion | flops 524288 | bytes 4194304 | tf_op jit(solution)/shard_map/stack | solution.py:101
  312.7 30.5 %copy.169 = f32[8,16,512,2,4]{1,0,4,3,2:T(8,128)} copy(f32[8,16,512,2,4]{0,4,2,1,3:T(4,128)} %pad_maximum_fusion.1) | data formatting | bytes 4194304 | tf_op jit(solution)/shard_map/stack | solution.py:101
  343.1 9.6 %copy.170 = f32[8,16,4096]{2,1,0:T(8,128)S(1)} copy(f32[8,16,4096]{1,0,2:T(8,128)} %bitcast.223) | data formatting | bytes 4194304 | tf_op jit(solution)/shard_map/reshape | solution.py:102
  352.8 29.4 %all_to_all.66 = f32[8,16,4096]{2,1,0:T(8,128)S(1)} all-to-all(f32[8,16,4096]{2,1,0:T(8,128)S(1)} %copy.170), channel_id=1, replica_groups=mesh['seq'=8,'pipe'=4] {'seq'}, dimensions={0} | all-to-all | bytes 4194304 | tf_op jit(solution)/shard_map/all_to_all | solution.py:211
  389.9 8.4 reduce.1
  399.8 18.8 %all_to_all.67 = bf16[8,2,32768]{2,1,0:T(2,128)(2,1)S(1)} all-to-all(bf16[8,2,32768]{2,1,0:T(2,128)(2,1)} %reshape.482), channel_id=1, replica_groups=mesh['seq'=8,'pipe'=4] {'seq'}, dimensions={0} | all-to-all | bytes 2097152 | tf_op jit(solution)/shard_map/all_to_all | solution.py:184
  429.5 10.6 %reshape.450 = f32[8,16,512,2,4]{1,0,4,3,2:T(8,128)} reshape(f32[1,128,4096]{1,2,0:T(8,128)} %copy.139) | data formatting | bytes 4194304 | tf_op jit(solution)/shard_map/convert_element_type | solution.py:185
  440.0 11.1 %fusion.169 = (f32[8,16,512,1,4]{1,0,4,3,2:T(8,128)}, f32[8,16,512,1,4]{1,0,4,3,2:T(8,128)}) fusion(f32[8,16,512,2,4]{1,0,4,3,2:T(8,128)} %reshape.450), kind=kLoop, calls=%fused_computation.302 | loop fusion | bytes 4194304 | tf_op jit(solution)/shard_map/slice | solution.py:92
  479.5 7.8 collective-permute-done.2
  488.2 31.8 %collective-permute-done.3 = f32[2,2,16,2048]{3,2,1,0:T(8,128)S(1)} collective-permute-done((f32[2,2,16,2048]{3,2,1,0:T(8,128)S(1)}, f32[2,2,16,2048]{3,2,1,0:T(8,128)S(1)}, u32[]{:S(2)}, u32[]{:S(2)}) %collective-permute-start.3) | collective-permute-done | bytes 524320 | tf_op jit(solution)/shard_map/ppermute | solution.py:27
  534.5 8.5 fusion.15
  556.2 7.3 copy.148
  563.6 53.1 %all_to_all.68 = f32[2,2,128,2048]{3,0,1,2:T(2,128)S(1)} all-to-all(f32[2,2,128,2048]{3,0,1,2:T(2,128)} %copy.148), channel_id=1, replica_groups=mesh['seq'=8,'pipe'=4] {'seq'}, dimensions={2} | all-to-all | bytes 8388608 | tf_op jit(solution)/shard_map/all_to_all | solution.py:206
  625.2 9.2 %copy.151 = f32[8,32768]{0,1:T(8,128)} copy(f32[8,32768]{1,0:T(8,128)} %get-tuple-element.51) | data formatting | bytes 2097152 | tf_op jit(solution)/shard_map/slice | solution.py:101
  634.4 8.9 %copy.152 = f32[8,32768]{0,1:T(8,128)} copy(f32[8,32768]{1,0:T(8,128)S(1)} %get-tuple-element.52) | data formatting | bytes 2097152 | tf_op jit(solution)/shard_map/slice | solution.py:101
  643.2 22.6 %pad_maximum_fusion = f32[8,16,512,2,4]{0,4,2,1,3:T(4,128)} fusion(f32[8,16,512,1,4]{0,4,2,1,3:T(4,128)} %bitcast.228, f32[8,16,512,1,4]{0,4,2,1,3:T(4,128)} %bitcast.226), kind=kLoop, calls=%fused_computation.2 | loop fusion | flops 524288 | bytes 4194304 | tf_op jit(solution)/shard_map/stack | solution.py:101
  665.8 30.5 %copy.153 = f32[8,16,512,2,4]{1,0,4,3,2:T(8,128)} copy(f32[8,16,512,2,4]{0,4,2,1,3:T(4,128)} %pad_maximum_fusion) | data formatting | bytes 4194304 | tf_op jit(solution)/shard_map/stack | solution.py:101
  696.3 10.6 %copy.154 = f32[8,16,4096]{2,1,0:T(8,128)} copy(f32[8,16,4096]{1,0,2:T(8,128)} %bitcast.224) | data formatting | bytes 4194304 | tf_op jit(solution)/shard_map/reshape | solution.py:102
  718.2 19.8 %all-to-all-done.2 = f32[8,16,4096]{2,1,0:T(8,128)} async-done(((f32[8,16,4096]{2,1,0:T(8,128)}), f32[8,16,4096]{2,1,0:T(8,128)}, u32[]{:S(2)}, u32[]{:S(2)}) %all-to-all-start.2) | async-done | bytes 2097184 | tf_op jit(solution)/shard_map/all_to_all | solution.py:211
  751.0 9.4 %multiply_reduce_fusion.2 = (f32[3,4096]{1,0:T(4,128)S(1)}, f32[3,4096]{1,0:T(4,128)S(1)}, f32[3,4096]{1,0:T(4,128)S(1)}, bf16[3,128,4096]{2,1,0:T(8,128)(2,1)}) fusion(f32[3,130,4096]{2,1,0:T(8,128)S(1)} %bitcast.222, f32[1,128,4096]{2,1,0:T(8,128)} %get-tuple-element.14, f32[1,128,4096]{2,1,0:T(8,128)S(1)} %get-tuple-element.13, ...), kind=kLoop, calls=%fused_computation.45 | loop fusion | flops 21983232 | bytes 41189376 | tf_op jit(solution)/shard_map/reduce_sum | solution.py:232
  775.1 38.3 %reduce-scatter.2.cloned.1.call-done = f32[128,256]{1,0:T(8,128)} async-done(((f32[1024,256]{1,0:T(8,128)}), f32[128,256]{1,0:T(8,128)}) %reduce-scatter.2.cloned.1.call-update) | async-done | bytes 131088 | tf_op jit(solution)/shard_map/reduce_scatter | solution.py:240
  814.9 55.2 %all-reduce.2.cloned.1.call-done = f32[3,3,4096]{2,1,0:T(4,128)} async-done(((f32[3,3,4096]{2,1,0:T(4,128)}), f32[3,3,4096]{2,1,0:T(4,128)}) %all-reduce.2.cloned.1.call-update) | async-done | bytes 147472 | tf_op jit(solution)/shard_map/psum | solution.py:237
  (249 shorter events, 260.1 us)
Async XLA Ops:
  7.2 13.3 %copy-start.31 = (f32[1,3,3,4096]{3,0,2,1:T(1,128)S(1)}, f32[1,3,3,4096]{3,0,2,1:T(1,128)}, u32[]{:S(2)}) copy-start(f32[1,3,3,4096]{3,0,2,1:T(1,128)} %param.11) | copy-start | bytes 442372
  7.2 170.6 %all-gather.3.cloned.1.call-start = ((), (), s32[]{:S(2)}) async-start(), calls=%async_computation.9 | async-start | bytes 1179648 | tf_op jit(solution)/shard_map/all_gather | solution.py:176
  11.4 10.0 %collective-permute-start = (bf16[3,2,4096]{2,1,0:T(2,128)(2,1)}, bf16[3,2,4096]{2,1,0:T(2,128)(2,1)}, u32[]{:S(2)}, u32[]{:S(2)}) collective-permute-start(bf16[3,2,4096]{2,1,0:T(2,128)(2,1)} %slice.194), channel_id=1, source_target_pairs={{0,4},{4,8},{8,12},{12,16},{16,20},{20,24},{24,28},{1,5},{5,9},{9,... | collective-permute-start | bytes 147464 | tf_op jit(solution)/shard_map/ppermute | solution.py:35
  40.2 20.0 %all-to-all-start.3 = ((bf16[8,2,32768]{2,1,0:T(2,128)(2,1)}), bf16[8,2,32768]{2,1,0:T(2,128)(2,1)S(1)}, u32[]{:S(2)}, u32[]{:S(2)}) async-start(bf16[8,2,32768]{2,1,0:T(2,128)(2,1)} %reshape.484), calls=%async_computation.3 | async-start | bytes 2097152 | tf_op jit(solution)/shard_map/all_to_all | solution.py:184
  48.2 135.8 %copy-start.35 = (s32[256]{0:T(256)}, s32[256]{0:T(256)S(1)}, u32[]{:S(2)}) copy-start(s32[256]{0:T(256)S(1)} %add_bitcast_fusion) | copy-start | bytes 3076
  107.6 7.2 collective-permute-start.8
  107.8 61.3 %copy-start.14 = (f32[2,128,2,128]{3,2,1,0:T(2,128)}, f32[2,128,2,128]{3,2,1,0:T(2,128)S(1)}, u32[]{:S(2)}) copy-start(f32[2,128,2,128]{3,2,1,0:T(2,128)S(1)} %reshape.442) | copy-start | bytes 786436
  108.0 87.1 %copy-start.12 = (f32[2,128,2,128]{3,2,1,0:T(2,128)}, f32[2,128,2,128]{3,2,1,0:T(2,128)S(1)}, u32[]{:S(2)}) copy-start(f32[2,128,2,128]{3,2,1,0:T(2,128)S(1)} %reshape.443) | copy-start | bytes 786436
  108.0 27.8 %copy-start.25 = (f32[2,2,16,2048]{3,2,1,0:T(8,128)S(1)}, f32[2,2,16,2048]{3,2,1,0:T(8,128)}, u32[]{:S(2)}) copy-start(f32[2,2,16,2048]{3,2,1,0:T(8,128)} %get-tuple-element.36) | copy-start | bytes 1572868
  109.2 50.7 %collective-permute-start.13 = (f32[2,2,16,2048]{3,2,1,0:T(8,128)S(1)}, f32[2,2,16,2048]{3,2,1,0:T(8,128)S(1)}, u32[]{:S(2)}, u32[]{:S(2)}) collective-permute-start(f32[2,2,16,2048]{3,2,1,0:T(8,128)S(1)} %fusion.70), channel_id=1, source_target_pairs={{0,24},{4,28},{8,16},{12,20},{16,8},{20,12},{24,0},{28,4},{1,25},{... | collective-permute-start | bytes 1572872 | tf_op jit(solution)/shard_map/ppermute | solution.py:27
  110.4 25.4 %collective-permute-start.9 = (f32[2,2,16,2048]{3,2,1,0:T(8,128)S(1)}, f32[2,2,16,2048]{3,2,1,0:T(8,128)S(1)}, u32[]{:S(2)}, u32[]{:S(2)}) collective-permute-start(f32[2,2,16,2048]{3,2,1,0:T(8,128)S(1)} %copy-done.28), channel_id=1, source_target_pairs={{0,8},{4,12},{8,0},{12,4},{16,24},{20,28},{24,16},{28,20},{1,9},{5... | collective-permute-start | bytes 1572872 | tf_op jit(solution)/shard_map/ppermute | solution.py:27
  112.6 48.1 %collective-permute-start.14 = (f32[2,2,16,2048]{3,2,1,0:T(8,128)S(1)}, f32[2,2,16,2048]{3,2,1,0:T(8,128)S(1)}, u32[]{:S(2)}, u32[]{:S(2)}) collective-permute-start(f32[2,2,16,2048]{3,2,1,0:T(8,128)S(1)} %copy-done.24), channel_id=1, source_target_pairs={{0,28},{4,24},{8,20},{12,16},{16,12},{20,8},{24,4},{28,0},{1,29},{... | collective-permute-start | bytes 1572872 | tf_op jit(solution)/shard_map/ppermute | solution.py:27
  113.2 44.2 %collective-permute-start.10 = (f32[2,2,16,2048]{3,2,1,0:T(8,128)S(1)}, f32[2,2,16,2048]{3,2,1,0:T(8,128)S(1)}, u32[]{:S(2)}, u32[]{:S(2)}) collective-permute-start(f32[2,2,16,2048]{3,2,1,0:T(8,128)S(1)} %copy-done.27), channel_id=1, source_target_pairs={{0,12},{4,8},{8,4},{12,0},{16,28},{20,24},{24,20},{28,16},{1,13},{... | collective-permute-start | bytes 1572872 | tf_op jit(solution)/shard_map/ppermute | solution.py:27
  114.9 43.4 %collective-permute-start.11 = (f32[2,2,16,2048]{3,2,1,0:T(8,128)S(1)}, f32[2,2,16,2048]{3,2,1,0:T(8,128)S(1)}, u32[]{:S(2)}, u32[]{:S(2)}) collective-permute-start(f32[2,2,16,2048]{3,2,1,0:T(8,128)S(1)} %copy-done.26), channel_id=1, source_target_pairs={{0,16},{4,20},{8,24},{12,28},{16,0},{20,4},{24,8},{28,12},{1,17},{... | collective-permute-start | bytes 1572872 | tf_op jit(solution)/shard_map/ppermute | solution.py:27
  135.8 23.3 %collective-permute-start.12 = (f32[2,2,16,2048]{3,2,1,0:T(8,128)S(1)}, f32[2,2,16,2048]{3,2,1,0:T(8,128)S(1)}, u32[]{:S(2)}, u32[]{:S(2)}) collective-permute-start(f32[2,2,16,2048]{3,2,1,0:T(8,128)S(1)} %copy-done.25), channel_id=1, source_target_pairs={{0,20},{4,16},{8,28},{12,24},{16,4},{20,0},{24,12},{28,8},{1,21},{... | collective-permute-start | bytes 1572872 | tf_op jit(solution)/shard_map/ppermute | solution.py:27
  177.8 13.2 %copy-start.33 = (s32[2048]{0:T(1024)S(1)}, s32[2048]{0:T(1024)}, u32[]{:S(2)}) copy-start(s32[2048]{0:T(1024)} %add_select_fusion.3) | copy-start | bytes 24580
  184.1 8.9 %copy-start.1 = (f32[2,2,128,2048]{2,3,0,1:T(8,128)S(1)}, f32[2,2,128,2048]{2,3,0,1:T(8,128)}, u32[]{:S(2)}) copy-start(f32[2,2,128,2048]{2,3,0,1:T(8,128)} %fusion.18) | copy-start | bytes 12582916
  208.6 53.9 %all-to-all-start.4 = ((f32[2,2,128,2048]{3,0,1,2:T(2,128)}), f32[2,2,128,2048]{3,0,1,2:T(2,128)}, u32[]{:S(2)}, u32[]{:S(2)}) async-start(f32[2,2,128,2048]{3,0,1,2:T(2,128)} %copy.164), calls=%async_computation.4 | async-start | bytes 8388608 | tf_op jit(solution)/shard_map/all_to_all | solution.py:206
  472.4 5.7 collective-permute-start.1
  472.5 14.9 %collective-permute-start.2 = (f32[2,2,16,2048]{3,2,1,0:T(8,128)S(1)}, f32[2,2,16,2048]{3,2,1,0:T(8,128)S(1)}, u32[]{:S(2)}, u32[]{:S(2)}) collective-permute-start(f32[2,2,16,2048]{3,2,1,0:T(8,128)S(1)} %get-tuple-element.41), channel_id=1, source_target_pairs={{0,8},{4,12},{8,0},{12,4},{16,24},{20,28},{24,16},{28,20},{1,9},{5... | collective-permute-start | bytes 1572872 | tf_op jit(solution)/shard_map/ppermute | solution.py:27
  474.0 51.3 %collective-permute-start.6 = (f32[2,2,16,2048]{3,2,1,0:T(8,128)S(1)}, f32[2,2,16,2048]{3,2,1,0:T(8,128)S(1)}, u32[]{:S(2)}, u32[]{:S(2)}) collective-permute-start(f32[2,2,16,2048]{3,2,1,0:T(8,128)S(1)} %fusion.87), channel_id=1, source_target_pairs={{0,24},{4,28},{8,16},{12,20},{16,8},{20,12},{24,0},{28,4},{1,25},{... | collective-permute-start | bytes 1572872 | tf_op jit(solution)/shard_map/ppermute | solution.py:27
  475.5 50.7 %collective-permute-start.7 = (f32[2,2,16,2048]{3,2,1,0:T(8,128)S(1)}, f32[2,2,16,2048]{3,2,1,0:T(8,128)S(1)}, u32[]{:S(2)}, u32[]{:S(2)}) collective-permute-start(f32[2,2,16,2048]{3,2,1,0:T(8,128)S(1)} %get-tuple-element.39), channel_id=1, source_target_pairs={{0,28},{4,24},{8,20},{12,16},{16,12},{20,8},{24,4},{28,0},{1,29},{... | collective-permute-start | bytes 1572872 | tf_op jit(solution)/shard_map/ppermute | solution.py:27
  476.4 43.6 %collective-permute-start.3 = (f32[2,2,16,2048]{3,2,1,0:T(8,128)S(1)}, f32[2,2,16,2048]{3,2,1,0:T(8,128)S(1)}, u32[]{:S(2)}, u32[]{:S(2)}) collective-permute-start(f32[2,2,16,2048]{3,2,1,0:T(8,128)S(1)} %get-tuple-element.42), channel_id=1, source_target_pairs={{0,12},{4,8},{8,4},{12,0},{16,28},{20,24},{24,20},{28,16},{1,13},{... | collective-permute-start | bytes 1572872 | tf_op jit(solution)/shard_map/ppermute | solution.py:27
  478.1 42.7 %collective-permute-start.4 = (f32[2,2,16,2048]{3,2,1,0:T(8,128)S(1)}, f32[2,2,16,2048]{3,2,1,0:T(8,128)S(1)}, u32[]{:S(2)}, u32[]{:S(2)}) collective-permute-start(f32[2,2,16,2048]{3,2,1,0:T(8,128)S(1)} %get-tuple-element.43), channel_id=1, source_target_pairs={{0,16},{4,20},{8,24},{12,28},{16,0},{20,4},{24,8},{28,12},{1,17},{... | collective-permute-start | bytes 1572872 | tf_op jit(solution)/shard_map/ppermute | solution.py:27
  487.3 37.1 %collective-permute-start.5 = (f32[2,2,16,2048]{3,2,1,0:T(8,128)S(1)}, f32[2,2,16,2048]{3,2,1,0:T(8,128)S(1)}, u32[]{:S(2)}, u32[]{:S(2)}) collective-permute-start(f32[2,2,16,2048]{3,2,1,0:T(8,128)S(1)} %get-tuple-element.44), channel_id=1, source_target_pairs={{0,20},{4,16},{8,28},{12,24},{16,4},{20,0},{24,12},{28,8},{1,21},{... | collective-permute-start | bytes 1572872 | tf_op jit(solution)/shard_map/ppermute | solution.py:27
  706.9 31.1 %all-to-all-start.2 = ((f32[8,16,4096]{2,1,0:T(8,128)}), f32[8,16,4096]{2,1,0:T(8,128)}, u32[]{:S(2)}, u32[]{:S(2)}) async-start(f32[8,16,4096]{2,1,0:T(8,128)} %copy.154), calls=%async_computation.2 | async-start | bytes 4194304 | tf_op jit(solution)/shard_map/all_to_all | solution.py:211
  711.4 26.6 %copy-start.11 = (bf16[1,128,4096]{2,1,0:T(8,128)(2,1)S(1)}, bf16[1,128,4096]{2,1,0:T(8,128)(2,1)}, u32[]{:S(2)}) copy-start(bf16[1,128,4096]{2,1,0:T(8,128)(2,1)} %param.9) | copy-start | bytes 3145732
  711.4 102.0 %reduce-scatter.2.cloned.1.call-start = ((), (), s32[]{:S(2)}) async-start(), calls=%async_computation.7 | async-start | bytes 1179648 | tf_op jit(solution)/shard_map/reduce_scatter | solution.py:240
  742.5 3.1 collective-permute-start.15
  751.0 11.0 %copy-start.36 = (s32[256]{0:T(256)S(1)}, s32[256]{0:T(256)}, u32[]{:S(2)}) copy-start(s32[256]{0:T(256)} %copy-done.35) | copy-start | bytes 3076
  760.4 111.5 %collective-permute-start.16 = (bf16[3,128,4096]{2,1,0:T(8,128)(2,1)}, bf16[3,128,4096]{2,1,0:T(8,128)(2,1)S(1)}, u32[]{:S(2)}, u32[]{:S(2)}) collective-permute-start(bf16[3,128,4096]{2,1,0:T(8,128)(2,1)} %get-tuple-element.19), channel_id=1, source_target_pairs={{1,0},{2,1},{3,2},{5,4},{6,5},{7,6},{9,8},{10,9},{11,10},{13,12},{... | collective-permute-start | bytes 9437192 | tf_op jit(solution)/shard_map/ppermute | solution.py:35
  774.1 96.1 %all-reduce.2.cloned.1.call-start = ((), (), s32[]{:S(2)}) async-start(), calls=%async_computation.8 | async-start | bytes 393216 | tf_op jit(solution)/shard_map/psum | solution.py:237
  (32 other events, 130.3 us)
Sparse Core Ops, SparseCore 0:
  9.9 26.1 all-gather.2
  774.2 39.1 reduce-scatter.1
  816.4 53.6 all-reduce.1
